TPU v7x, 32 devices: a whole 2x2x4 slice. The times are simulated.
32 devices in a mesh: groups: 2 (over y), span: 4 (over x, core), head: 4 (over z).
Axes of the slice: x: 2, y: 2, z: 4, core: 2. Of those that a mesh axis runs over, the one named last changes fastest.
Arguments:
- queries: bfloat16 [4096, 1024], P(('groups', 'span', 'head')), parts along dimension 0, may hold values from -8 to 8
- keys: bfloat16 [4096, 1024], P(('groups', 'span', 'head')), parts along dimension 0, may hold values from -8 to 8
- values: bfloat16 [4096, 1024], P(('groups', 'span', 'head')), parts along dimension 0, may hold values from -6 to 6
- tile_offsets: int32 [32, 7], P(('groups', 'span')), parts along dimension 0, may hold values from 0 to 6, as said below
- timesteps: int32 [8], P(('groups', 'span')), parts along dimension 0, may hold values from 0 to 999
- time_weight: bfloat16 [256, 1024], P(None, 'head'), may hold values from -0.375 to 0.375
Outputs:
- attended: bfloat16 [4096, 1024], P(('groups', 'span', 'head')), parts along dimension 0
There are 2 independent parts, one for each index of `groups`. A program takes and returns all parts, laid end to end along the dimension named above; an argument that names none is the same for every part. Nothing has to cross between parts.
Inputs may be any that keep to these rules, and one draw needn't show every extreme that they name: `tile_offsets`: the first entry of each row is 0 and the 7 entries of a row are distinct.
All inputs are finite; a program needn't handle non-finite values.
Results may differ from a plain program's by a relative error of at most 0.0035.
Values may be sent and summed in bfloat16 or wider, within the bound.
No kernel may reach another device: no remote copies, remote signals or barrier semaphores. Data moves between devices by JAX's collectives and lax.ppermute only.
A program may use at most 64 MiB of HBM per device.

v0:
```python
import math
import jax
import jax.numpy as jnp
from jax import lax
from jax.sharding import PartitionSpec as P

HEAD_SIZE = 128
TILE = 128
FREQ = 256


def shifted(value, axis, by):
    size = lax.axis_size(axis)
    pairs = [(i, i + by) for i in range(size) if 0 <= i + by < size]
    return lax.ppermute(value, axis, pairs)


def local(queries, keys, values, tile_offsets, timesteps, time_weight):
    query_heads, key_heads, value_heads = (
        lax.all_to_all(queries, "head", split_axis=1, concat_axis=0, tiled=True),
        lax.all_to_all(keys, "head", split_axis=1, concat_axis=0, tiled=True),
        lax.all_to_all(values, "head", split_axis=1, concat_axis=0, tiled=True),
    )
    span_rows = query_heads.shape[0]
    width = query_heads.shape[1]
    heads_here = width // HEAD_SIZE
    tiles_here = span_rows // TILE
    reach = 3 * tiles_here // 2
    listed = tile_offsets.shape[1]
    tail_rows = (reach - tiles_here) * TILE
    resident = jnp.concatenate([key_heads, value_heads], axis=1)
    nearer = shifted(resident, "span", 1)
    farther = shifted(resident[span_rows - tail_rows :], "span", 2)
    window = jnp.concatenate([farther, nearer, resident], axis=0)
    window = window.reshape(reach + tiles_here, TILE, 2 * width)
    half = FREQ // 2
    freqs = jnp.exp(-math.log(10000.0) * jnp.arange(half, dtype=jnp.float32) / half)
    angles = timesteps.astype(jnp.float32)[:, None] * freqs[None, :]
    embedded = jnp.concatenate([jnp.cos(angles), jnp.sin(angles)], axis=1)
    gate = jnp.dot(embedded, time_weight.astype(jnp.float32), precision=lax.Precision.HIGHEST)
    gate_rows = gate.reshape(1, 1, heads_here, HEAD_SIZE)
    position = lax.axis_index("span")
    scale = HEAD_SIZE ** (-0.5)
    query_blocks = query_heads.reshape(tiles_here // 4, 4, TILE, heads_here, HEAD_SIZE)
    offset_blocks = tile_offsets.reshape(tiles_here // 4, 4, listed)

    def one_block(inputs):
        block, query_part, offsets = inputs
        local_tiles = block * 4 + jnp.arange(4, dtype=jnp.int32)
        source = local_tiles[:, None] - offsets
        usable = position * tiles_here + source >= 0
        picked = window[source + reach].reshape(4, listed * TILE, 2 * width)
        key_part = picked[:, :, :width].reshape(4, listed * TILE, heads_here, HEAD_SIZE)
        value_part = picked[:, :, width:].reshape(4, listed * TILE, heads_here, HEAD_SIZE)
        scores = (
            jnp.einsum("qthd,qkhd->qhtk", query_part, key_part, preferred_element_type=jnp.float32)
            * scale
        )
        keep = jnp.repeat(usable, TILE, axis=1)
        scores = jnp.where(keep[:, None, None, :], scores, -1e30)
        top = jnp.max(scores, axis=-1, keepdims=True)
        weights = jnp.exp(scores - top)
        total = jnp.sum(weights, axis=-1, keepdims=True)
        rounded = weights.astype(jnp.bfloat16)
        mixed = jnp.einsum(
            "qhtk,qkhd->qthd", rounded, value_part, preferred_element_type=jnp.float32
        )
        mixed = mixed / jnp.transpose(total, (0, 2, 1, 3))
        return (mixed * (1.0 + gate_rows)).astype(jnp.bfloat16)

    blocks = jnp.arange(tiles_here // 4, dtype=jnp.int32)
    gated = lax.map(one_block, (blocks, query_blocks, offset_blocks)).reshape(span_rows, width)
    return lax.all_to_all(gated, "head", split_axis=0, concat_axis=1, tiled=True)


def solution(mesh):
    return jax.shard_map(
        local,
        mesh=mesh,
        in_specs=(
            P(("groups", "span", "head"), None),
            P(("groups", "span", "head"), None),
            P(("groups", "span", "head"), None),
            P(("groups", "span"), None),
            P(("groups", "span")),
            P(None, "head"),
        ),
        out_specs=P(("groups", "span", "head"), None),
        check_vma=False,
    )
```

profile of v0, /device:TPU:7, one launch (start us, length us, event | category | flops | bytes accessed | tf_op | source)
XLA Modules:
  0.0 76.2 jit_solution(9081810094877849396)
XLA Ops:
  0.0 1.8 %copy.18 = bf16[128,1024]{0,1:T(8,128)(2,1)} copy(bf16[128,1024]{1,0:T(8,128)(2,1)} %param.8) | data formatting | bytes 524288 | tf_op args[2]
  1.8 4.6 %all-to-all-start.1 = ((bf16[128,4,256]{0,2,1:T(8,128)(2,1)}), bf16[128,4,256]{0,2,1:T(8,128)(2,1)S(1)}, u32[]{:S(2)}, u32[]{:S(2)}) async-start(bf16[128,4,256]{0,2,1:T(8,128)(2,1)} %bitcast.3), calls=%async_computation.1 | async-start | bytes 524288 | tf_op jit(solution)/shard_map/all_to_all | solution.py:22
  6.4 1.8 %copy.16 = bf16[128,1024]{0,1:T(8,128)(2,1)} copy(bf16[128,1024]{1,0:T(8,128)(2,1)} %param.7) | data formatting | bytes 524288 | tf_op args[1]
  8.2 0.7 add_compare_fusion
  8.9 5.1 %all-to-all-done.1 = bf16[128,4,256]{0,2,1:T(8,128)(2,1)S(1)} async-done(((bf16[128,4,256]{0,2,1:T(8,128)(2,1)}), bf16[128,4,256]{0,2,1:T(8,128)(2,1)S(1)}, u32[]{:S(2)}, u32[]{:S(2)}) %all-to-all-start.1) | async-done | bytes 262176 | tf_op jit(solution)/shard_map/all_to_all | solution.py:22
  14.0 3.4 %all-to-all-start = ((bf16[128,4,256]{0,2,1:T(8,128)(2,1)}), bf16[128,4,256]{0,2,1:T(8,128)(2,1)S(1)}, u32[]{:S(2)}, u32[]{:S(2)}) async-start(bf16[128,4,256]{0,2,1:T(8,128)(2,1)} %bitcast), calls=%async_computation | async-start | bytes 524288 | tf_op jit(solution)/shard_map/all_to_all | solution.py:21
  17.4 0.1 broadcast_bitcast_fusion
  17.5 1.8 %copy.22 = bf16[128,1024]{0,1:T(8,128)(2,1)} copy(bf16[128,1024]{1,0:T(8,128)(2,1)} %param.6) | data formatting | bytes 524288 | tf_op args[0]
  19.9 0.1 fusion.27
  20.0 0.1 fusion.22
  20.1 0.2 copy.19
  20.3 2.7 %all-to-all-done = bf16[128,4,256]{0,2,1:T(8,128)(2,1)S(1)} async-done(((bf16[128,4,256]{0,2,1:T(8,128)(2,1)}), bf16[128,4,256]{0,2,1:T(8,128)(2,1)S(1)}, u32[]{:S(2)}, u32[]{:S(2)}) %all-to-all-start) | async-done | bytes 262176 | tf_op jit(solution)/shard_map/all_to_all | solution.py:21
  23.0 3.4 %all-to-all-start.2 = ((bf16[128,4,256]{0,2,1:T(8,128)(2,1)}), bf16[128,4,256]{0,2,1:T(8,128)(2,1)S(1)}, u32[]{:S(2)}, u32[]{:S(2)}) async-start(bf16[128,4,256]{0,2,1:T(8,128)(2,1)} %bitcast.10), calls=%async_computation.2 | async-start | bytes 524288 | tf_op jit(solution)/shard_map/all_to_all | solution.py:20
  26.4 0.1 copy.17
  26.6 1.3 %collective-permute-start.1 = (bf16[512,512]{1,0:T(8,128)(2,1)S(1)}, bf16[512,512]{1,0:T(8,128)(2,1)S(1)}, u32[]{:S(2)}, u32[]{:S(2)}) collective-permute-start(bf16[512,512]{1,0:T(8,128)(2,1)S(1)} %pad_maximum_fusion), channel_id=1, source_target_pairs={{0,4},{4,8},{8,12},{1,5},{5,9},{9,13},{2,6},{6,10},{10,14},{3,7},{... | collective-permute-start | bytes 1572872 | tf_op jit(solution)/shard_map/ppermute | solution.py:15
  27.9 0.0 copy-done.2
  27.9 0.1 reshape.97
  28.1 1.3 %collective-permute-start = (bf16[256,512]{1,0:T(8,128)(2,1)S(1)}, bf16[256,512]{1,0:T(8,128)(2,1)S(1)}, u32[]{:S(2)}, u32[]{:S(2)}) collective-permute-start(bf16[256,512]{1,0:T(8,128)(2,1)S(1)} %fusion.21), channel_id=1, source_target_pairs={{0,8},{4,12},{1,9},{5,13},{2,10},{6,14},{3,11},{7,15},{16,24},{20,... | collective-permute-start | bytes 786440 | tf_op jit(solution)/shard_map/ppermute | solution.py:15
  29.4 16.3 %collective-permute-done = bf16[256,512]{1,0:T(8,128)(2,1)S(1)} collective-permute-done((bf16[256,512]{1,0:T(8,128)(2,1)S(1)}, bf16[256,512]{1,0:T(8,128)(2,1)S(1)}, u32[]{:S(2)}, u32[]{:S(2)}) %collective-permute-start) | collective-permute-done | bytes 262176 | tf_op jit(solution)/shard_map/ppermute | solution.py:15
  45.7 0.0 collective-permute-done.1
  45.7 0.1 maximum_maximum_fusion
  45.8 2.6 %gather_fusion = bf16[28,128,512]{2,1,0:T(8,128)(2,1)} fusion(bf16[10,128,512]{2,1,0:T(8,128)(2,1)S(1)} %bitcast.73, s32[1024]{0:T(1024)S(1)} %pad_clamp_fusion), kind=kCustom, calls=%fused_computation | custom fusion | bytes 7340144 | tf_op jit(solution)/shard_map/while/body/eval_jaxpr/gather | solution.py:52
  48.5 3.6 %fusion.32 = (bf16[4,896,256]{2,1,0:T(8,128)(2,1)S(1)}, bf16[4,896,256]{2,1,0:T(8,128)(2,1)}) fusion(bf16[4,896,512]{2,1,0:T(8,128)(2,1)} %bitcast.74), kind=kLoop, calls=%fused_computation.40 | loop fusion | bytes 7340032 | tf_op jit(solution)/shard_map/while/body/eval_jaxpr/slice | solution.py:53
  52.0 3.6 %copy.20 = bf16[4,896,256]{1,2,0:T(8,128)(2,1)} copy(bf16[4,896,256]{2,1,0:T(8,128)(2,1)} %get-tuple-element.18) | data formatting | bytes 3670016 | tf_op jit(solution)/shard_map/while/body/eval_jaxpr/slice | solution.py:54
  55.6 2.4 %copy.21 = bf16[4,896,256]{1,2,0:T(8,128)(2,1)} copy(bf16[4,896,256]{2,1,0:T(8,128)(2,1)S(1)} %get-tuple-element.17) | data formatting | bytes 3670016 | tf_op jit(solution)/shard_map/while/body/eval_jaxpr/slice | solution.py:53
  58.0 0.0 all-to-all-done.2
  58.0 2.6 %bitcast_reduce_fusion = (f32[4,2,128]{2,1,0:T(2,128)S(1)}, f32[4,2,896,128]{3,2,1,0:T(8,128)S(1)}) fusion(pred[4,896]{1,0:T(4,128)(4,1)S(1)} %bitcast.88, bf16[4,896,2,128]{1,3,2,0:T(8,128)(2,1)} %bitcast.75, bf16[4,128,2,128]{1,3,2,0:T(8,128)(2,1)S(1)} %bitcast.86), kind=kOutput, calls=%fused_computation.2 | convolution fusion | flops 237632512 | bytes 5774848 | tf_op jit(solution)/shard_map/while/body/eval_jaxpr/qthd,qkhd->qhtk/dot_general | solution.py:56
  60.6 1.1 %fusion.1 = f32[4,2,128]{2,1,0:T(2,128)S(1)} fusion(f32[4,2,896,128]{3,2,1,0:T(8,128)S(1)} %get-tuple-element.20, f32[4,2,128]{2,1,0:T(2,128)S(1)} %get-tuple-element.19, pred[4,896]{1,0:T(4,128)(4,1)S(1)} %bitcast.89), kind=kLoop, calls=%fused_computation.5 | loop fusion | flops 3668992 | bytes 3681792 | tf_op jit(solution)/shard_map/while/body/eval_jaxpr/reduce_sum | solution.py:63
  61.7 0.0 copy-done.1
  61.7 1.3 %fusion.18 = bf16[4,128,2,128]{1,3,2,0:T(8,128)(2,1)S(1)} fusion(bf16[4,896,2,128]{1,3,2,0:T(8,128)(2,1)S(1)} %bitcast.82, f32[4,2,896,128]{3,2,1,0:T(8,128)S(1)} %get-tuple-element.20, f32[4,2,128]{2,1,0:T(2,128)S(1)} %get-tuple-element.19, pred[4,896]{1,0:T(4,128)(4,1)S(1)} %bitcast.90, f32[2,128]{1,0:T(2,128)S(1)} %broadcast_add_fusion, ...), kind=kOutput, calls=%fused_computation.16 | convolution fusion | flops 238944256 | bytes 5779968 | tf_op jit(solution)/shard_map/while/body/eval_jaxpr/qhtk,qkhd->qthd/dot_general | solution.py:65
  63.0 12.3 %all_to_all.73 = bf16[4,128,256]{1,2,0:T(8,128)(2,1)S(1)} all-to-all(bf16[4,128,256]{1,2,0:T(8,128)(2,1)S(1)} %bitcast.87), channel_id=1, replica_groups=mesh['groups'=2,'span'=4,'head'=4] {'head'}, dimensions={0} | all-to-all | bytes 524288 | tf_op jit(solution)/shard_map/all_to_all | solution.py:73
  75.4 0.8 %copy.32 = bf16[128,1024]{1,0:T(8,128)(2,1)} copy(bf16[128,1024]{0,1:T(8,128)(2,1)S(1)} %bitcast.85) | data formatting | bytes 524288 | tf_op jit(solution)/shard_map/all_to_all | solution.py:73
  (10 shorter events, 0.1 us)
Async XLA Ops:
  0.0 20.0 %copy-start = (bf16[256,256]{1,0:T(8,128)(2,1)S(1)}, bf16[256,256]{1,0:T(8,128)(2,1)}, u32[]{:S(2)}) copy-start(bf16[256,256]{1,0:T(8,128)(2,1)} %param.11) | copy-start | bytes 393220
  0.0 27.9 %copy-start.2 = (s32[4,7]{1,0:T(4,128)S(1)}, s32[4,7]{1,0:T(4,128)}, u32[]{:S(2)}) copy-start(s32[4,7]{1,0:T(4,128)} %param.9) | copy-start | bytes 340
  1.8 12.2 %all-to-all-start.1 = ((bf16[128,4,256]{0,2,1:T(8,128)(2,1)}), bf16[128,4,256]{0,2,1:T(8,128)(2,1)S(1)}, u32[]{:S(2)}, u32[]{:S(2)}) async-start(bf16[128,4,256]{0,2,1:T(8,128)(2,1)} %bitcast.3), calls=%async_computation.1 | async-start | bytes 524288 | tf_op jit(solution)/shard_map/all_to_all | solution.py:22
  14.0 9.0 %all-to-all-start = ((bf16[128,4,256]{0,2,1:T(8,128)(2,1)}), bf16[128,4,256]{0,2,1:T(8,128)(2,1)S(1)}, u32[]{:S(2)}, u32[]{:S(2)}) async-start(bf16[128,4,256]{0,2,1:T(8,128)(2,1)} %bitcast), calls=%async_computation | async-start | bytes 524288 | tf_op jit(solution)/shard_map/all_to_all | solution.py:21
  23.0 35.0 %all-to-all-start.2 = ((bf16[128,4,256]{0,2,1:T(8,128)(2,1)}), bf16[128,4,256]{0,2,1:T(8,128)(2,1)S(1)}, u32[]{:S(2)}, u32[]{:S(2)}) async-start(bf16[128,4,256]{0,2,1:T(8,128)(2,1)} %bitcast.10), calls=%async_computation.2 | async-start | bytes 524288 | tf_op jit(solution)/shard_map/all_to_all | solution.py:20
  26.6 19.1 %collective-permute-start.1 = (bf16[512,512]{1,0:T(8,128)(2,1)S(1)}, bf16[512,512]{1,0:T(8,128)(2,1)S(1)}, u32[]{:S(2)}, u32[]{:S(2)}) collective-permute-start(bf16[512,512]{1,0:T(8,128)(2,1)S(1)} %pad_maximum_fusion), channel_id=1, source_target_pairs={{0,4},{4,8},{8,12},{1,5},{5,9},{9,13},{2,6},{6,10},{10,14},{3,7},{... | collective-permute-start | bytes 1572872 | tf_op jit(solution)/shard_map/ppermute | solution.py:15
  28.1 17.7 %collective-permute-start = (bf16[256,512]{1,0:T(8,128)(2,1)S(1)}, bf16[256,512]{1,0:T(8,128)(2,1)S(1)}, u32[]{:S(2)}, u32[]{:S(2)}) collective-permute-start(bf16[256,512]{1,0:T(8,128)(2,1)S(1)} %fusion.21), channel_id=1, source_target_pairs={{0,8},{4,12},{1,9},{5,13},{2,10},{6,14},{3,11},{7,15},{16,24},{20,... | collective-permute-start | bytes 786440 | tf_op jit(solution)/shard_map/ppermute | solution.py:15
  58.0 3.8 %copy-start.1 = (bf16[4,896,256]{1,2,0:T(8,128)(2,1)S(1)}, bf16[4,896,256]{1,2,0:T(8,128)(2,1)}, u32[]{:S(2)}) copy-start(bf16[4,896,256]{1,2,0:T(8,128)(2,1)} %copy.20) | copy-start | bytes 5505028
where the time goes:
time: 76.8 us; the launch traced here: 76.2 us
  waiting for transfers between devices  24.1 us (31%)
  local copies, waits for them, and re-layouts  18.9 us (25%)
  starting transfers between devices  14 us (18%)
  blocking collectives  12.3 us (16%)
  matrix products  4.02 us (5%)
  other arithmetic  2.02 us (3%)
  between operations  0.81 us (1%)
    ppermute x2, waiting for transfers between devices, shifted(): return lax.ppermute(value, axis, pairs)  16.3 us
    all_to_all x1, blocking collectives, local(): lax.all_to_all(gated, 'head', split_axis=0, concat_axis=1, tiled=True)  12.3 us
    slice x2, local copies, waits for them, and re-layouts, one_block(): picked[:, :, :width].reshape(4, listed * TILE, heads_here, HEAD_SIZE)  5.92 us
    unnamed x11, local copies, waits for them, and re-layouts  5.49 us
    all_to_all x1, waiting for transfers between devices, local(): lax.all_to_all(values, 'head', split_axis=1, concat_axis=0, tiled=True)  5.09 us
    all_to_all x1, starting transfers between devices, local(): lax.all_to_all(values, 'head', split_axis=1, concat_axis=0, tiled=True)  4.59 us
    slice x1, local copies, waits for them, and re-layouts, one_block(): picked[:, :, width:].reshape(4, listed * TILE, heads_here, HEAD_SIZE)  3.6 us
    all_to_all x1, starting transfers between devices, local(): lax.all_to_all(queries, 'head', split_axis=1, concat_axis=0, tiled=True)  3.41 us
  transfers between devices with their start and end apart: 5, of which 3 were waited for; matrix products, arithmetic and copies ran while one was open for 23% of the time, Pallas kernels for 0%

commit v1 on v0

--- a/solution.py
+++ b/solution.py
@@ -16,9 +16,33 @@
 
 
 def local(queries, keys, values, tile_offsets, timesteps, time_weight):
+
+    def make_positions(t0):
+        named_axis = "head"
+        q_next = lax.axis_size(named_axis)
+        tile_out = lax.axis_index(named_axis)
+        b_next, high = (q_next, tile_out)
+        current_value = t0.shape[1] // b_next
+        reached = list(t0.shape)
+        reached[1] = current_value
+        v_now = reached[0]
+        reached[0] = v_now * b_next
+        piece_now = jnp.zeros(reached, t0.dtype)
+        for jj in range(b_next):
+            u_next = lax.dynamic_slice_in_dim(
+                t0, (high ^ jj) * current_value, current_value, axis=1
+            )
+            if jj:
+                a_now = tuple(((it, it ^ jj) for it in range(b_next)))
+                u_next = lax.ppermute(u_next, named_axis, a_now)
+            piece_now = lax.dynamic_update_slice_in_dim(
+                piece_now, u_next, (high ^ jj) * v_now, axis=0
+            )
+        return piece_now
+
     query_heads, key_heads, value_heads = (
         lax.all_to_all(queries, "head", split_axis=1, concat_axis=0, tiled=True),
-        lax.all_to_all(keys, "head", split_axis=1, concat_axis=0, tiled=True),
+        make_positions(keys),
         lax.all_to_all(values, "head", split_axis=1, concat_axis=0, tiled=True),
     )
     span_rows = query_heads.shape[0]

time: 76.8 us -> 71.3 us (0.928)
  waiting for transfers between devices: 24.1 us -> 18.6 us
  local copies, waits for them, and re-layouts: 18.9 us -> 17.9 us
  starting transfers between devices: 14 us -> 15 us
    all_to_all x1, waiting for transfers between devices: 5.09 us -> 0.01 us  [local(): lax.all_to_all(values, 'head', split_axis=1, concat_axis=0, tiled=True)]
    ppermute x0 -> x3, starting transfers between devices: none -> 3.69 us  [make_positions(): u_next = lax.ppermute(u_next, named_axis, a_now)]
    all_to_all x1 -> x0, starting transfers between devices: 3.4 us -> none  [local(): lax.all_to_all(keys, 'head', split_axis=1, concat_axis=0, tiled=True)]
    ppermute x0 -> x3, waiting for transfers between devices: none -> 3.34 us  [make_positions(): u_next = lax.ppermute(u_next, named_axis, a_now)]
    all_to_all x1 -> x0, waiting for transfers between devices: 2.69 us -> none  [local(): lax.all_to_all(keys, 'head', split_axis=1, concat_axis=0, tiled=True)]
    unnamed x11 -> x10, local copies, waits for them, and re-layouts: 5.49 us -> 3.77 us
    ppermute x2, waiting for transfers between devices: 16.3 us -> 15.3 us  [shifted(): return lax.ppermute(value, axis, pairs)]
    dynamic_slice x0 -> x1, local copies, waits for them, and re-layouts: none -> 0.97 us  [make_positions(): lax.dynamic_slice_in_dim(t0, (high ^ jj) * current_value, current_value,...]
  transfers between devices with their start and end apart: 5 -> 7, of which waited for: 3 -> 3; matrix products, arithmetic and copies ran while one was open for 23% -> 23% of each run, Pallas kernels for 0% -> 0%
where the time goes in v1:
time: 71.3 us; the launch traced here: 70.7 us
  waiting for transfers between devices  18.6 us (26%)
  local copies, waits for them, and re-layouts  17.9 us (25%)
  starting transfers between devices  15 us (21%)
  blocking collectives  12.3 us (17%)
  matrix products  4.02 us (6%)
  other arithmetic  2.02 us (3%)
  between operations  0.81 us (1%)
    ppermute x2, waiting for transfers between devices, shifted(): return lax.ppermute(value, axis, pairs)  15.3 us
    all_to_all x1, blocking collectives, local(): lax.all_to_all(gated, 'head', split_axis=0, concat_axis=1, tiled=True)  12.3 us
    slice x2, local copies, waits for them, and re-layouts, one_block(): picked[:, :, :width].reshape(4, listed * TILE, heads_here, HEAD_SIZE)  5.89 us
    all_to_all x1, starting transfers between devices, local(): lax.all_to_all(values, 'head', split_axis=1, concat_axis=0, tiled=True)  4.59 us
    all_to_all x1, starting transfers between devices, local(): lax.all_to_all(queries, 'head', split_axis=1, concat_axis=0, tiled=True)  4.1 us
    unnamed x10, local copies, waits for them, and re-layouts  3.77 us
    ppermute x3, starting transfers between devices, make_positions(): u_next = lax.ppermute(u_next, named_axis, a_now)  3.69 us
    slice x1, local copies, waits for them, and re-layouts, one_block(): picked[:, :, width:].reshape(4, listed * TILE, heads_here, HEAD_SIZE)  3.56 us
  transfers between devices with their start and end apart: 7, of which 3 were waited for; matrix products, arithmetic and copies ran while one was open for 23% of the time, Pallas kernels for 0%

profile of v1, /device:TPU:7, one launch (start us, length us, event | category | flops | bytes accessed | tf_op | source)
XLA Modules:
  0.0 70.7 jit_solution(9458985991420652630)
XLA Ops:
  0.0 1.8 %copy.16 = bf16[128,1024]{0,1:T(8,128)(2,1)} copy(bf16[128,1024]{1,0:T(8,128)(2,1)} %param.8) | data formatting | bytes 524288 | tf_op args[2]
  1.8 4.6 %all-to-all-start = ((bf16[128,4,256]{0,2,1:T(8,128)(2,1)}), bf16[128,4,256]{0,2,1:T(8,128)(2,1)S(1)}, u32[]{:S(2)}, u32[]{:S(2)}) async-start(bf16[128,4,256]{0,2,1:T(8,128)(2,1)} %bitcast), calls=%async_computation | async-start | bytes 524288 | tf_op jit(solution)/shard_map/all_to_all | solution.py:46
  6.4 1.0 %constant_dynamic-slice_fusion = (bf16[128,256]{1,0:T(8,128)(2,1)S(1)}, bf16[128,256]{1,0:T(8,128)(2,1)S(1)}, bf16[512,256]{1,0:T(8,128)(2,1)S(1)}, bf16[128,256]{1,0:T(8,128)(2,1)S(1)}) fusion(bf16[128,1024]{1,0:T(8,128)(2,1)} %param.7, s32[]{:T(128)S(6)} %select_n.46, s32[]{:T(128)S(6)} %select_n.42, bf16[512,256]{1,0:T(8,128)(2,1)S(1)} %broadcast_in_dim.41, ...), kind=kLoop, calls=%fused_computation.32 | loop fusion | bytes 524308 | tf_op jit(solution)/shard_map/dynamic_slice | solution.py:32
  7.4 1.5 %collective-permute-start = (bf16[128,256]{1,0:T(8,128)(2,1)S(1)}, bf16[128,256]{1,0:T(8,128)(2,1)S(1)}, u32[]{:S(2)}, u32[]{:S(2)}) collective-permute-start(bf16[128,256]{1,0:T(8,128)(2,1)S(1)} %get-tuple-element.20), channel_id=1, source_target_pairs={{0,1},{1,0},{2,3},{3,2},{4,5},{5,4},{6,7},{7,6},{8,9},{9,8},{10,11... | collective-permute-start | bytes 196616 | tf_op jit(solution)/shard_map/ppermute | solution.py:37
  8.9 2.1 %collective-permute-start.1 = (bf16[128,256]{1,0:T(8,128)(2,1)S(1)}, bf16[128,256]{1,0:T(8,128)(2,1)S(1)}, u32[]{:S(2)}, u32[]{:S(2)}) collective-permute-start(bf16[128,256]{1,0:T(8,128)(2,1)S(1)} %get-tuple-element.30), channel_id=1, source_target_pairs={{0,2},{1,3},{2,0},{3,1},{4,6},{5,7},{6,4},{7,5},{8,10},{9,11},{10,... | collective-permute-start | bytes 196616 | tf_op jit(solution)/shard_map/ppermute | solution.py:37
  11.0 0.1 collective-permute-start.2
  11.8 0.1 fusion.27
  11.8 0.7 add_compare_fusion
  12.5 0.1 fusion.22
  12.7 0.1 broadcast_bitcast_fusion
  12.7 1.9 %copy.20 = bf16[128,1024]{0,1:T(8,128)(2,1)} copy(bf16[128,1024]{1,0:T(8,128)(2,1)} %param.6) | data formatting | bytes 524288 | tf_op args[0]
  14.6 0.0 collective-permute-done
  14.6 2.6 %collective-permute-done.1 = bf16[128,256]{1,0:T(8,128)(2,1)S(1)} collective-permute-done((bf16[128,256]{1,0:T(8,128)(2,1)S(1)}, bf16[128,256]{1,0:T(8,128)(2,1)S(1)}, u32[]{:S(2)}, u32[]{:S(2)}) %collective-permute-start.1) | collective-permute-done | bytes 65568 | tf_op jit(solution)/shard_map/ppermute | solution.py:37
  17.2 0.8 %collective-permute-done.2 = bf16[128,256]{1,0:T(8,128)(2,1)S(1)} collective-permute-done((bf16[128,256]{1,0:T(8,128)(2,1)S(1)}, bf16[128,256]{1,0:T(8,128)(2,1)S(1)}, u32[]{:S(2)}, u32[]{:S(2)}) %collective-permute-start.2) | collective-permute-done | bytes 65568 | tf_op jit(solution)/shard_map/ppermute | solution.py:37
  18.0 0.0 all-to-all-done
  18.0 4.1 %all-to-all-start.1 = ((bf16[128,4,256]{0,2,1:T(8,128)(2,1)}), bf16[128,4,256]{0,2,1:T(8,128)(2,1)S(1)}, u32[]{:S(2)}, u32[]{:S(2)}) async-start(bf16[128,4,256]{0,2,1:T(8,128)(2,1)} %bitcast.7), calls=%async_computation.1 | async-start | bytes 524288 | tf_op jit(solution)/shard_map/all_to_all | solution.py:44
  22.1 0.1 copy.17
  22.3 1.3 %collective-permute-start.4 = (bf16[512,512]{1,0:T(8,128)(2,1)S(1)}, bf16[512,512]{1,0:T(8,128)(2,1)S(1)}, u32[]{:S(2)}, u32[]{:S(2)}) collective-permute-start(bf16[512,512]{1,0:T(8,128)(2,1)S(1)} %pad_maximum_fusion), channel_id=1, source_target_pairs={{0,4},{4,8},{8,12},{1,5},{5,9},{9,13},{2,6},{6,10},{10,14},{3,7},{... | collective-permute-start | bytes 1572872 | tf_op jit(solution)/shard_map/ppermute | solution.py:15
  23.6 0.1 reshape.94
  23.7 1.3 %collective-permute-start.3 = (bf16[256,512]{1,0:T(8,128)(2,1)S(1)}, bf16[256,512]{1,0:T(8,128)(2,1)S(1)}, u32[]{:S(2)}, u32[]{:S(2)}) collective-permute-start(bf16[256,512]{1,0:T(8,128)(2,1)S(1)} %fusion.21), channel_id=1, source_target_pairs={{0,8},{4,12},{1,9},{5,13},{2,10},{6,14},{3,11},{7,15},{16,24},{20,... | collective-permute-start | bytes 786440 | tf_op jit(solution)/shard_map/ppermute | solution.py:15
  25.0 15.3 %collective-permute-done.3 = bf16[256,512]{1,0:T(8,128)(2,1)S(1)} collective-permute-done((bf16[256,512]{1,0:T(8,128)(2,1)S(1)}, bf16[256,512]{1,0:T(8,128)(2,1)S(1)}, u32[]{:S(2)}, u32[]{:S(2)}) %collective-permute-start.3) | collective-permute-done | bytes 262176 | tf_op jit(solution)/shard_map/ppermute | solution.py:15
  40.3 0.0 collective-permute-done.4
  40.3 0.1 maximum_maximum_fusion
  40.4 2.6 %gather_fusion = bf16[28,128,512]{2,1,0:T(8,128)(2,1)} fusion(bf16[10,128,512]{2,1,0:T(8,128)(2,1)S(1)} %bitcast.70, s32[1024]{0:T(1024)S(1)} %pad_clamp_fusion), kind=kCustom, calls=%fused_computation | custom fusion | bytes 7340144 | tf_op jit(solution)/shard_map/while/body/eval_jaxpr/gather | solution.py:76
  43.0 3.6 %fusion.32 = (bf16[4,896,256]{2,1,0:T(8,128)(2,1)S(1)}, bf16[4,896,256]{2,1,0:T(8,128)(2,1)}) fusion(bf16[4,896,512]{2,1,0:T(8,128)(2,1)} %bitcast.71), kind=kLoop, calls=%fused_computation.47 | loop fusion | bytes 7340032 | tf_op jit(solution)/shard_map/while/body/eval_jaxpr/slice | solution.py:77
  46.6 3.6 %copy.18 = bf16[4,896,256]{1,2,0:T(8,128)(2,1)} copy(bf16[4,896,256]{2,1,0:T(8,128)(2,1)} %get-tuple-element.18) | data formatting | bytes 3670016 | tf_op jit(solution)/shard_map/while/body/eval_jaxpr/slice | solution.py:78
  50.2 2.3 %copy.19 = bf16[4,896,256]{1,2,0:T(8,128)(2,1)} copy(bf16[4,896,256]{2,1,0:T(8,128)(2,1)S(1)} %get-tuple-element.17) | data formatting | bytes 3670016 | tf_op jit(solution)/shard_map/while/body/eval_jaxpr/slice | solution.py:77
  52.5 2.6 %bitcast_reduce_fusion = (f32[4,2,128]{2,1,0:T(2,128)S(1)}, f32[4,2,896,128]{3,2,1,0:T(8,128)S(1)}) fusion(pred[4,896]{1,0:T(4,128)(4,1)S(1)} %bitcast.81, bf16[4,896,2,128]{1,3,2,0:T(8,128)(2,1)} %bitcast.72, bf16[4,128,2,128]{1,3,2,0:T(8,128)(2,1)S(1)} %bitcast.79), kind=kOutput, calls=%fused_computation.2 | convolution fusion | flops 237632512 | bytes 5774848 | tf_op jit(solution)/shard_map/while/body/eval_jaxpr/qthd,qkhd->qhtk/dot_general | solution.py:80
  55.1 1.1 %fusion.1 = f32[4,2,128]{2,1,0:T(2,128)S(1)} fusion(f32[4,2,896,128]{3,2,1,0:T(8,128)S(1)} %get-tuple-element.33, f32[4,2,128]{2,1,0:T(2,128)S(1)} %get-tuple-element.32, pred[4,896]{1,0:T(4,128)(4,1)S(1)} %bitcast.82), kind=kLoop, calls=%fused_computation.5 | loop fusion | flops 3668992 | bytes 3681792 | tf_op jit(solution)/shard_map/while/body/eval_jaxpr/reduce_sum | solution.py:87
  56.3 1.3 %fusion.18 = bf16[4,128,2,128]{1,3,2,0:T(8,128)(2,1)S(1)} fusion(bf16[4,896,2,128]{1,3,2,0:T(8,128)(2,1)S(1)} %bitcast.76, f32[4,2,896,128]{3,2,1,0:T(8,128)S(1)} %get-tuple-element.33, f32[4,2,128]{2,1,0:T(2,128)S(1)} %get-tuple-element.32, pred[4,896]{1,0:T(4,128)(4,1)S(1)} %bitcast.83, f32[2,128]{1,0:T(2,128)S(1)} %broadcast_add_fusion, ...), kind=kOutput, calls=%fused_computation.16 | convolution fusion | flops 238944256 | bytes 5779968 | tf_op jit(solution)/shard_map/while/body/eval_jaxpr/qhtk,qkhd->qthd/dot_general | solution.py:89
  57.5 12.3 %all_to_all.54 = bf16[4,128,256]{1,2,0:T(8,128)(2,1)S(1)} all-to-all(bf16[4,128,256]{1,2,0:T(8,128)(2,1)S(1)} %bitcast.80), channel_id=1, replica_groups=mesh['groups'=2,'span'=4,'head'=4] {'head'}, dimensions={0} | all-to-all | bytes 524288 | tf_op jit(solution)/shard_map/all_to_all | solution.py:97
  69.9 0.8 %copy.30 = bf16[128,1024]{1,0:T(8,128)(2,1)} copy(bf16[128,1024]{0,1:T(8,128)(2,1)S(1)} %bitcast.78) | data formatting | bytes 524288 | tf_op jit(solution)/shard_map/all_to_all | solution.py:97
  (17 shorter events, 0.1 us)
Async XLA Ops:
  0.0 12.5 %copy-start = (bf16[256,256]{1,0:T(8,128)(2,1)S(1)}, bf16[256,256]{1,0:T(8,128)(2,1)}, u32[]{:S(2)}) copy-start(bf16[256,256]{1,0:T(8,128)(2,1)} %param.11) | copy-start | bytes 393220
  0.0 23.6 %copy-start.2 = (s32[4,7]{1,0:T(4,128)S(1)}, s32[4,7]{1,0:T(4,128)}, u32[]{:S(2)}) copy-start(s32[4,7]{1,0:T(4,128)} %param.9) | copy-start | bytes 340
  1.8 16.1 %all-to-all-start = ((bf16[128,4,256]{0,2,1:T(8,128)(2,1)}), bf16[128,4,256]{0,2,1:T(8,128)(2,1)S(1)}, u32[]{:S(2)}, u32[]{:S(2)}) async-start(bf16[128,4,256]{0,2,1:T(8,128)(2,1)} %bitcast), calls=%async_computation | async-start | bytes 524288 | tf_op jit(solution)/shard_map/all_to_all | solution.py:46
  7.4 7.2 %collective-permute-start = (bf16[128,256]{1,0:T(8,128)(2,1)S(1)}, bf16[128,256]{1,0:T(8,128)(2,1)S(1)}, u32[]{:S(2)}, u32[]{:S(2)}) collective-permute-start(bf16[128,256]{1,0:T(8,128)(2,1)S(1)} %get-tuple-element.20), channel_id=1, source_target_pairs={{0,1},{1,0},{2,3},{3,2},{4,5},{5,4},{6,7},{7,6},{8,9},{9,8},{10,11... | collective-permute-start | bytes 196616 | tf_op jit(solution)/shard_map/ppermute | solution.py:37
  8.9 8.2 %collective-permute-start.1 = (bf16[128,256]{1,0:T(8,128)(2,1)S(1)}, bf16[128,256]{1,0:T(8,128)(2,1)S(1)}, u32[]{:S(2)}, u32[]{:S(2)}) collective-permute-start(bf16[128,256]{1,0:T(8,128)(2,1)S(1)} %get-tuple-element.30), channel_id=1, source_target_pairs={{0,2},{1,3},{2,0},{3,1},{4,6},{5,7},{6,4},{7,5},{8,10},{9,11},{10,... | collective-permute-start | bytes 196616 | tf_op jit(solution)/shard_map/ppermute | solution.py:37
  11.0 6.9 %collective-permute-start.2 = (bf16[128,256]{1,0:T(8,128)(2,1)S(1)}, bf16[128,256]{1,0:T(8,128)(2,1)S(1)}, u32[]{:S(2)}, u32[]{:S(2)}) collective-permute-start(bf16[128,256]{1,0:T(8,128)(2,1)S(1)} %get-tuple-element.19), channel_id=1, source_target_pairs={{0,3},{1,2},{2,1},{3,0},{4,7},{5,6},{6,5},{7,4},{8,11},{9,10},{10,... | collective-permute-start | bytes 196616 | tf_op jit(solution)/shard_map/ppermute | solution.py:37
  18.0 34.5 %all-to-all-start.1 = ((bf16[128,4,256]{0,2,1:T(8,128)(2,1)}), bf16[128,4,256]{0,2,1:T(8,128)(2,1)S(1)}, u32[]{:S(2)}, u32[]{:S(2)}) async-start(bf16[128,4,256]{0,2,1:T(8,128)(2,1)} %bitcast.7), calls=%async_computation.1 | async-start | bytes 524288 | tf_op jit(solution)/shard_map/all_to_all | solution.py:44
  22.3 18.1 %collective-permute-start.4 = (bf16[512,512]{1,0:T(8,128)(2,1)S(1)}, bf16[512,512]{1,0:T(8,128)(2,1)S(1)}, u32[]{:S(2)}, u32[]{:S(2)}) collective-permute-start(bf16[512,512]{1,0:T(8,128)(2,1)S(1)} %pad_maximum_fusion), channel_id=1, source_target_pairs={{0,4},{4,8},{8,12},{1,5},{5,9},{9,13},{2,6},{6,10},{10,14},{3,7},{... | collective-permute-start | bytes 1572872 | tf_op jit(solution)/shard_map/ppermute | solution.py:15
  23.7 16.6 %collective-permute-start.3 = (bf16[256,512]{1,0:T(8,128)(2,1)S(1)}, bf16[256,512]{1,0:T(8,128)(2,1)S(1)}, u32[]{:S(2)}, u32[]{:S(2)}) collective-permute-start(bf16[256,512]{1,0:T(8,128)(2,1)S(1)} %fusion.21), channel_id=1, source_target_pairs={{0,8},{4,12},{1,9},{5,13},{2,10},{6,14},{3,11},{7,15},{16,24},{20,... | collective-permute-start | bytes 786440 | tf_op jit(solution)/shard_map/ppermute | solution.py:15
  52.5 3.8 %copy-start.1 = (bf16[4,896,256]{1,2,0:T(8,128)(2,1)S(1)}, bf16[4,896,256]{1,2,0:T(8,128)(2,1)}, u32[]{:S(2)}) copy-start(bf16[4,896,256]{1,2,0:T(8,128)(2,1)} %copy.18) | copy-start | bytes 5505028
